TPU v7x, 256 devices: a whole 4x4x8 slice. The times are simulated.
256 devices in a mesh: rep: 8 (over z_lo, y), inner: 32 (over z_hi, x, core).
Axes of the slice: x: 4, y: 4, z: 8 (z_hi: 4, z_lo: 2; z = z_hi * 2 + z_lo), core: 2. Of those that a mesh axis runs over, the one named last changes fastest.
Arguments:
- local_weights: float32 [8, 12, 1600, 1600], P('rep', None, 'inner'), may hold values from -6 to 6
- owner_global: float32 [32, 1600, 1600], P('inner', None, 'rep'), may hold values from -6 to 6
- owner_momentum: float32 [32, 1600, 1600], P('inner', None, 'rep'), may hold values from -6 to 6
- owner_list: int32 [12], replicated, may hold values from 0 to 31, as said below
- local_down: float32 [8, 6400, 1600], P('rep', 'inner'), may hold values from -6 to 6
- global_down: float32 [6400, 1600], P('inner', 'rep'), may hold values from -6 to 6
- down_basis: float32 [6400, 64], P('inner'), may hold values from -0.15625 to 0.15625
- coef_momentum: float32 [64, 1600], P(None, 'rep'), may hold values from -6 to 6
Outputs:
- new_weights: float32 [12, 1600, 1600], P(None, 'inner')
- momentum_out: float32 [32, 1600, 1600], P('inner', None, 'rep')
- new_down: float32 [6400, 1600], P('inner', 'rep')
- coef_new: float32 [64, 1600], P(None, 'rep')
Inputs may be any that keep to these rules, and one draw needn't show every extreme that they name: `owner_list`: the 12 entries are distinct inner indices; both ends of the range are owners.
All inputs are finite; a program needn't handle non-finite values.
Results may differ from a plain program's by a relative error of at most 0.00007.
Values sent between devices are 32-bit elements; how exact they have to be, the bound alone decides.
A program may use at most 128 MiB of HBM per device.

v0:
```python
import jax
import jax.numpy as jnp
from jax import lax
from jax.sharding import PartitionSpec as P

outer_momentum = 0.9
outer_rate = 0.7


def project_rows(basis, values):
    return lax.dot_general(
        basis,
        values,
        (((0,), (0,)), ((), ())),
        precision=lax.Precision.HIGHEST,
        preferred_element_type=jnp.float32,
    )


def on_device(
    local_weights,
    owner_global,
    owner_momentum,
    owner_list,
    local_down,
    global_down,
    down_basis,
    coef_momentum,
):
    groups = lax.axis_size("rep")
    owners = lax.axis_size("inner")
    inner_index = lax.axis_index("inner")
    width = global_down.shape[1]
    col_start = lax.axis_index("rep") * width
    block = local_weights[0]
    matrices = block.shape[0]
    slab = block.shape[1]
    order = jnp.arange(matrices, dtype=jnp.int32)
    match = (owner_list[None, :] == jnp.arange(owners, dtype=jnp.int32)[:, None]).astype(jnp.int32)
    owned = (jnp.sum(match, axis=1) > 0).astype(jnp.float32)
    picked = jnp.sum(match * order[None, :], axis=1)
    down_local = project_rows(down_basis, local_down[0])
    down_global = project_rows(down_basis, global_down)
    summed = lax.psum_scatter(block, "rep", scatter_dimension=2, tiled=True)
    placed = lax.dynamic_update_slice_in_dim(jnp.zeros_like(down_local), down_global, col_start, 1)
    total = lax.psum(placed - down_local / groups, ("rep", "inner"))
    coef_step = lax.dynamic_slice_in_dim(total, col_start, width, 1)
    average = summed / groups
    current = owner_global[0]
    moment = owner_momentum[0]
    outgoing = average[picked] * owned[:, None, None]
    arrived = lax.all_to_all(outgoing, "inner", split_axis=0, concat_axis=0, tiled=True).reshape(
        owners * slab, width
    )
    delta = current - arrived
    moment_new = outer_momentum * moment + delta
    theta = current - outer_rate * (delta + outer_momentum * moment_new)
    is_owner = jnp.sum((owner_list == inner_index).astype(jnp.float32))
    momentum_out = (moment_new * is_owner)[None]
    returned = lax.all_to_all(
        theta.reshape(owners, slab, width), "inner", split_axis=0, concat_axis=0, tiled=True
    )
    updated = returned[owner_list]
    new_weights = lax.all_gather(updated, "rep", axis=2, tiled=True)
    coef_new = outer_momentum * coef_momentum + coef_step
    change = jnp.dot(
        down_basis,
        coef_step + outer_momentum * coef_new,
        precision=lax.Precision.HIGHEST,
        preferred_element_type=jnp.float32,
    )
    new_down = global_down - outer_rate * change
    return (new_weights, momentum_out, new_down, coef_new)


def solution(mesh):
    in_specs = (
        P("rep", None, "inner", None),
        P("inner", None, "rep"),
        P("inner", None, "rep"),
        P(),
        P("rep", "inner", None),
        P("inner", "rep"),
        P("inner", None),
        P(None, "rep"),
    )
    out_specs = (P(None, "inner", None), P("inner", None, "rep"), P("inner", "rep"), P(None, "rep"))
    return jax.shard_map(
        on_device, mesh=mesh, in_specs=in_specs, out_specs=out_specs, check_vma=False
    )
```

profile of v0, /device:TPU:4, one launch (start us, length us, event | category | flops | bytes accessed | tf_op | source)
XLA Modules:
  0.0 588.5 jit_solution(15279377533316422879)
XLA Ops:
  8.1 4.6 copy.44
  12.7 0.6 copy-done.7
  13.4 0.6 dynamic-slice
  14.7 117.2 %all-reduce.6.cloned.1.call-done = f32[12,50,1600]{2,1,0:T(8,128)} async-done(((f32[12,50,1600]{2,1,0:T(8,128)}), f32[12,50,1600]{2,1,0:T(8,128)}) %all-reduce.6.cloned.1.call-update) | async-done | bytes 3840016
  132.0 1.5 dynamic-slice_multiply_fusion
  133.4 1.9 gather_fusion
  135.3 2.9 broadcast_multiply_fusion
  138.2 9.2 %all-to-all-start = ((f32[32,50,200]{2,1,0:T(8,128)}), f32[32,50,200]{2,1,0:T(8,128)S(1)}, u32[]{:S(2)}, u32[]{:S(2)}) async-start(f32[32,50,200]{2,1,0:T(8,128)} %broadcast_multiply_fusion), calls=%async_computation | async-start | bytes 3670016 | tf_op jit(solution)/shard_map/all_to_all | solution.py:52
  147.5 3.0 copy.32
  150.5 3.0 copy.33
  153.5 2.6 squeeze.10
  156.1 0.6 fusion.8
  156.7 36.5 %all-to-all-done = f32[32,50,200]{2,1,0:T(8,128)S(1)} async-done(((f32[32,50,200]{2,1,0:T(8,128)}), f32[32,50,200]{2,1,0:T(8,128)S(1)}, u32[]{:S(2)}, u32[]{:S(2)}) %all-to-all-start) | async-done | bytes 1280032 | tf_op jit(solution)/shard_map/all_to_all | solution.py:52
  193.2 1.4 reshape.35
  194.6 5.1 add_multiply_fusion
  199.6 2.6 mul.65
  202.2 3.8 multiply_subtract_fusion
  206.1 5.1 all-to-all-start.1
  211.3 0.2 fusion.12
  211.5 0.8 broadcast_in_dim.5
  212.3 1.5 dynamic_update_slice.3
  213.8 2.7 fusion
  216.6 36.6 %all-to-all-done.1 = f32[32,50,200]{2,1,0:T(8,128)S(1)} async-done(((f32[32,50,200]{2,1,0:T(8,128)}), f32[32,50,200]{2,1,0:T(8,128)S(1)}, u32[]{:S(2)}, u32[]{:S(2)}) %all-to-all-start.1) | async-done | bytes 1280032 | tf_op jit(solution)/shard_map/all_to_all | solution.py:60
  253.2 1.4 gather_fusion.1
  254.6 3.1 copy.34
  257.7 0.8 copy.36
  258.5 307.0 %all-reduce.4.cloned.1.call-done = f32[64,1600]{1,0:T(8,128)} async-done(((f32[64,1600]{1,0:T(8,128)}), f32[64,1600]{1,0:T(8,128)}) %all-reduce.4.cloned.1.call-update) | async-done | bytes 409616 | tf_op jit(solution)/shard_map/psum | solution.py:46
  565.5 1.0 multiply_add_fusion
  566.5 1.4 fusion.3
  568.0 0.8 copy.39
  568.8 1.6 copy.38
  570.3 10.7 %copy.37 = f32[12,50,1600]{2,1,0:T(8,128)} copy(f32[12,50,1600]{1,0,2:T(8,128)} %all-gather.3.cloned.1.call-done) | data formatting | bytes 7680000
  (28 shorter events, 0.3 us)
Async XLA Ops:
  8.0 205.8 %copy-start = (f32[1,200,1600]{2,1,0:T(8,128)S(1)}, f32[1,200,1600]{2,1,0:T(8,128)}, u32[]{:S(2)}) copy-start(f32[1,200,1600]{2,1,0:T(8,128)} %param.12) | copy-start | bytes 3840004
  8.0 124.0 %all-reduce.6.cloned.1.call-start = ((), (), s32[]{:S(2)}) async-start(), calls=%async_computation.4 | async-start | bytes 8945664
  12.7 0.7 copy-start.7
  12.7 1.9 copy-start.6
  138.2 55.0 %all-to-all-start = ((f32[32,50,200]{2,1,0:T(8,128)}), f32[32,50,200]{2,1,0:T(8,128)S(1)}, u32[]{:S(2)}, u32[]{:S(2)}) async-start(f32[32,50,200]{2,1,0:T(8,128)} %broadcast_multiply_fusion), calls=%async_computation | async-start | bytes 3670016 | tf_op jit(solution)/shard_map/all_to_all | solution.py:52
  206.1 5.2 copy-start.2
  206.1 5.2 copy-start.3
  206.1 47.1 %all-to-all-start.1 = ((f32[32,50,200]{2,1,0:T(8,128)}), f32[32,50,200]{2,1,0:T(8,128)S(1)}, u32[]{:S(2)}, u32[]{:S(2)}) async-start(f32[32,50,200]{2,1,0:T(8,128)} %multiply_subtract_fusion), calls=%async_computation.1 | async-start | bytes 3670016 | tf_op jit(solution)/shard_map/all_to_all | solution.py:60
  211.2 354.3 %all-reduce.4.cloned.1.call-start = ((), (), s32[]{:S(2)}) async-start(), calls=%async_computation.2 | async-start | bytes 851968 | tf_op jit(solution)/shard_map/psum | solution.py:46
  216.5 353.8 %all-gather.3.cloned.1.call-start = ((), (), s32[]{:S(2)}) async-start(), calls=%async_computation.3 | async-start | bytes 14745600 | tf_op jit(solution)/shard_map/all_gather | solution.py:64
  254.6 310.9 %copy-start.5 = (f32[64,200]{1,0:T(8,128)S(1)}, f32[64,200]{1,0:T(8,128)}, u32[]{:S(2)}) copy-start(f32[64,200]{1,0:T(8,128)} %param.15) | copy-start | bytes 153604
  257.7 311.0 %copy-start.1 = (f32[1,1600,200]{2,1,0:T(8,128)S(1)}, f32[1,1600,200]{2,1,0:T(8,128)}, u32[]{:S(2)}) copy-start(f32[1,1600,200]{2,1,0:T(8,128)} %get-tuple-element.22) | copy-start | bytes 3840004
  566.5 3.8 copy-start.4
Sparse Core Ops, SparseCore 0:
  12.9 119.0 all-reduce.5
  257.9 139.3 all-gather.2
Sparse Core Ops, SparseCore 1:
  218.1 347.4 all-reduce.3
where the time goes:
time: 589 us; the launch traced here: 588 us
  waiting for transfers between devices  497 us (84%)
  local copies, waits for them, and re-layouts  41 us (7%)
  between operations  16.3 us (3%)
  other arithmetic  15 us (3%)
  starting transfers between devices  14.5 us (2%)
    psum x1, waiting for transfers between devices, on_device(): total = lax.psum(placed - down_local / groups, ('rep', 'inner'))  307 us
    unnamed x4, waiting for transfers between devices  117 us
    all_to_all x1, waiting for transfers between devices, on_device(): lax.all_to_all(theta.reshape(owners, slab, width), 'inner', split_axis=0,...  36.6 us
    all_to_all x1, waiting for transfers between devices, on_device(): lax.all_to_all(outgoing, 'inner', split_axis=0, concat_axis=0, tiled=True)  36.5 us
    unnamed x24, local copies, waits for them, and re-layouts  25.8 us
  transfers between devices with their start and end apart: 5, of which 4 were waited for; matrix products, arithmetic and copies ran while one was open for 4% of the time, Pallas kernels for 0%

commit v1 on v0

--- a/solution.py
+++ b/solution.py
@@ -43,7 +43,9 @@
     down_global = project_rows(down_basis, global_down)
     summed = lax.psum_scatter(block, "rep", scatter_dimension=2, tiled=True)
     placed = lax.dynamic_update_slice_in_dim(jnp.zeros_like(down_local), down_global, col_start, 1)
-    total = lax.psum(placed - down_local / groups, ("rep", "inner"))
+    total = placed - down_local / groups
+    for over in ("inner", "rep"):
+        total = lax.psum(total, over)
     coef_step = lax.dynamic_slice_in_dim(total, col_start, width, 1)
     average = summed / groups
     current = owner_global[0]

time: 589 us -> 701 us (1.19)
  waiting for transfers between devices: 497 us -> 612 us
    all_gather x1, waiting for transfers between devices: 0.01 us -> 130 us  [on_device(): new_weights = lax.all_gather(updated, 'rep', axis=2, tiled=True)]
    psum x1, waiting for transfers between devices: 307 us -> 270 us  [on_device(): total = lax.psum(total, over)]
    unnamed x4, waiting for transfers between devices: 117 us -> 130 us
    all_to_all x1, waiting for transfers between devices: 36.6 us -> 45.8 us  [on_device(): lax.all_to_all(theta.reshape(owners, slab, width), 'inner', split_axis=0,...]
    unnamed x24 -> x22, local copies, waits for them, and re-layouts: 25.8 us -> 25 us
  transfers between devices with their start and end apart: 5 -> 5, of which waited for: 4 -> 5; matrix products, arithmetic and copies ran while one was open for 4% -> 3% of each run, Pallas kernels for 0% -> 0%
where the time goes in v1:
time: 701 us; the launch traced here: 700 us
  waiting for transfers between devices  612 us (87%)
  local copies, waits for them, and re-layouts  38.7 us (6%)
  other arithmetic  15.2 us (2%)
  between operations  14.6 us (2%)
  starting transfers between devices  14.3 us (2%)
    psum x1, waiting for transfers between devices, on_device(): total = lax.psum(total, over)  270 us
    unnamed x4, waiting for transfers between devices  130 us
    all_gather x1, waiting for transfers between devices, on_device(): new_weights = lax.all_gather(updated, 'rep', axis=2, tiled=True)  130 us
    all_to_all x1, waiting for transfers between devices, on_device(): lax.all_to_all(theta.reshape(owners, slab, width), 'inner', split_axis=0,...  45.8 us
    all_to_all x1, waiting for transfers between devices, on_device(): lax.all_to_all(outgoing, 'inner', split_axis=0, concat_axis=0, tiled=True)  36.6 us
    unnamed x22, local copies, waits for them, and re-layouts  25 us
  transfers between devices with their start and end apart: 5, of which 5 were waited for; matrix products, arithmetic and copies ran while one was open for 3% of the time, Pallas kernels for 0%

profile of v1, /device:TPU:4, one launch (start us, length us, event | category | flops | bytes accessed | tf_op | source)
XLA Modules:
  0.0 699.7 jit_solution(12990792709297339533)
XLA Ops:
  7.2 1.3 fusion.12
  8.6 0.7 dynamic_update_slice.3
  9.2 2.5 fusion
  11.8 4.5 copy.44
  16.4 269.5 %all-reduce.5.cloned.1.call-done = f32[64,1600]{1,0:T(8,128)} async-done(((f32[64,1600]{1,0:T(8,128)}), f32[64,1600]{1,0:T(8,128)}) %all-reduce.5.cloned.1.call-update) | async-done | bytes 409616 | tf_op jit(solution)/shard_map/psum | solution.py:48
  285.9 0.6 copy-done.6
  286.6 0.6 dynamic-slice
  287.9 130.2 %all-reduce.7.cloned.1.call-done = (f32[12,50,1600]{2,1,0:T(8,128)}, f32[64,1600]{1,0:T(8,128)}) async-done(((f32[12,50,1600]{2,1,0:T(8,128)}, f32[64,1600]{1,0:T(8,128)}), (f32[12,50,1600]{2,1,0:T(8,128)}, f32[64,1600]{1,0:T(8,128)})) %all-reduce.7.cloned.1.call-update) | async-done | bytes 4249616
  418.2 1.5 dynamic-slice_multiply_fusion
  419.7 1.9 gather_fusion
  421.5 2.9 broadcast_multiply_fusion
  424.5 9.2 %all-to-all-start = ((f32[32,50,200]{2,1,0:T(8,128)}), f32[32,50,200]{2,1,0:T(8,128)S(1)}, u32[]{:S(2)}, u32[]{:S(2)}) async-start(f32[32,50,200]{2,1,0:T(8,128)} %broadcast_multiply_fusion), calls=%async_computation | async-start | bytes 3670016 | tf_op jit(solution)/shard_map/all_to_all | solution.py:54
  433.7 3.0 copy.32
  436.7 3.0 copy.33
  439.7 2.6 squeeze.10
  442.3 0.6 fusion.8
  442.9 36.6 %all-to-all-done = f32[32,50,200]{2,1,0:T(8,128)S(1)} async-done(((f32[32,50,200]{2,1,0:T(8,128)}), f32[32,50,200]{2,1,0:T(8,128)S(1)}, u32[]{:S(2)}, u32[]{:S(2)}) %all-to-all-start) | async-done | bytes 1280032 | tf_op jit(solution)/shard_map/all_to_all | solution.py:54
  479.4 1.4 reshape.35
  480.8 5.1 add_multiply_fusion
  485.9 2.6 mul.65
  488.5 3.8 multiply_subtract_fusion
  492.3 5.0 all-to-all-start.1
  497.4 45.8 %all-to-all-done.1 = f32[32,50,200]{2,1,0:T(8,128)S(1)} async-done(((f32[32,50,200]{2,1,0:T(8,128)}), f32[32,50,200]{2,1,0:T(8,128)S(1)}, u32[]{:S(2)}, u32[]{:S(2)}) %all-to-all-start.1) | async-done | bytes 1280032 | tf_op jit(solution)/shard_map/all_to_all | solution.py:62
  543.2 1.4 gather_fusion.1
  544.6 3.1 copy.34
  547.7 0.1 copy.36
  547.9 1.1 multiply_add_fusion
  549.0 1.4 fusion.3
  550.4 0.8 copy.39
  551.2 1.6 copy.38
  552.7 129.7 %all-gather.3.cloned.1.call-done = f32[12,50,1600]{1,0,2:T(8,128)} async-done(((f32[12,50,200]{1,0,2:T(8,128)}), f32[12,50,1600]{1,0,2:T(8,128)}) %all-gather.3.cloned.1.call-update) | async-done | bytes 3840016 | tf_op jit(solution)/shard_map/all_gather | solution.py:66
  682.4 10.7 %copy.37 = f32[12,50,1600]{2,1,0:T(8,128)} copy(f32[12,50,1600]{1,0,2:T(8,128)} %all-gather.3.cloned.1.call-done) | data formatting | bytes 7680000
  (26 shorter events, 0.4 us)
Async XLA Ops:
  7.2 2.1 copy-start
  7.2 278.7 %all-reduce.5.cloned.1.call-start = ((), (), s32[]{:S(2)}) async-start(), calls=%async_computation.2 | async-start | bytes 851968 | tf_op jit(solution)/shard_map/psum | solution.py:48
  11.8 406.4 %all-reduce.7.cloned.1.call-start = ((), (), s32[]{:S(2)}) async-start(), calls=%async_computation.4 | async-start | bytes 9797632
  285.9 0.7 copy-start.6
  285.9 1.9 copy-start.5
  424.5 55.0 %all-to-all-start = ((f32[32,50,200]{2,1,0:T(8,128)}), f32[32,50,200]{2,1,0:T(8,128)S(1)}, u32[]{:S(2)}, u32[]{:S(2)}) async-start(f32[32,50,200]{2,1,0:T(8,128)} %broadcast_multiply_fusion), calls=%async_computation | async-start | bytes 3670016 | tf_op jit(solution)/shard_map/all_to_all | solution.py:54
  492.3 50.8 %all-to-all-start.1 = ((f32[32,50,200]{2,1,0:T(8,128)}), f32[32,50,200]{2,1,0:T(8,128)S(1)}, u32[]{:S(2)}, u32[]{:S(2)}) async-start(f32[32,50,200]{2,1,0:T(8,128)} %multiply_subtract_fusion), calls=%async_computation.1 | async-start | bytes 3670016 | tf_op jit(solution)/shard_map/all_to_all | solution.py:62
  497.3 185.1 %all-gather.3.cloned.1.call-start = ((), (), s32[]{:S(2)}) async-start(), calls=%async_computation.3 | async-start | bytes 14745600 | tf_op jit(solution)/shard_map/all_gather | solution.py:66
  544.6 3.1 copy-start.2
  544.6 4.4 copy-start.3
  547.7 3.5 copy-start.1
  549.0 3.7 copy-start.4
Sparse Core Ops, SparseCore 0:
  11.9 273.9 all-reduce.4
  289.5 128.6 all-reduce.6
  547.9 134.5 all-gather.2
